TPU v7x, 32 devices: a whole 2x2x4 slice. The times are simulated.
32 devices in a mesh: groups: 2 (over y), seq: 16 (over z, x, core).
Axes of the slice: x: 2, y: 2, z: 4, core: 2. Of those that a mesh axis runs over, the one named last changes fastest.
Arguments:
- span_frames: bfloat16 [512, 512], P(('groups', 'seq')), parts along dimension 0, may hold values from -3 to 3
- query_rows: bfloat16 [512, 512], P(('groups', 'seq')), parts along dimension 0, may hold values from -12 to 12
- key_rows: bfloat16 [16384, 512], P(('groups', 'seq')), parts along dimension 0, may hold values from -6 to 6
- context_frames: bfloat16 [16384, 512], P(('groups', 'seq')), parts along dimension 0, may hold values from -6 to 6
- key_mask: int32 [16384], P(('groups', 'seq')), parts along dimension 0, may hold values from 0 to 1, as said below
- value_weight: bfloat16 [512, 512], replicated, may hold values from -0.5 to 0.5
- out_weight: bfloat16 [512, 512], replicated, may hold values from -0.25 to 0.25
- expand_weight: bfloat16 [512, 1024], replicated, may hold values from -0.25 to 0.25
- depth_weight: float32 [31, 512], replicated, may hold values from -1 to 1
- norm_scale: float32 [512], replicated, may hold values from 0.5 to 2
- norm_shift: float32 [512], replicated, may hold values from -3 to 3
- project_weight: bfloat16 [512, 512], replicated, may hold values from -0.25 to 0.25
Outputs:
- layer_out: bfloat16 [512, 512], P(('groups', 'seq')), parts along dimension 0
There are 2 independent parts, one for each index of `groups`. A program takes and returns all parts, laid end to end along the dimension named above; an argument that names none is the same for every part. Nothing has to cross between parts.
Inputs may be any that keep to these rules, and one draw needn't show every extreme that they name: `key_mask`: within each block of 512 frames held by one index of seq, the real frames come first and there is at least one.
All inputs are finite; a program needn't handle non-finite values.
Results may differ from a plain program's by a relative error of at most 0.013.
Values may be sent and summed in bfloat16 or wider, within the bound.
A program may use at most 384 MiB of HBM per device.

v0:
```python
import math
import jax
import jax.numpy as jnp
from jax import lax
from jax.sharding import PartitionSpec as P

HEADS = 8


def combined_all(value, axis, join):
    pieces = jax.tree.map(lambda part: lax.all_gather(part, axis), value)
    head = jax.tree.map(lambda part: part[0], pieces)
    tail = jax.tree.map(lambda part: part[1:], pieces)
    so_far, _ = lax.scan(lambda so_far, section: (join(so_far, section), None), head, tail)
    return so_far


def with_halo(block, sides, width):
    for axis, dim in sides:
        count = lax.axis_size(axis)
        forward = [(i, i + 1) for i in range(count - 1)]
        backward = [(target, source) for source, target in forward]
        low = lax.ppermute(
            lax.slice_in_dim(block, block.shape[dim] - width, None, axis=dim), axis, forward
        )
        high = lax.ppermute(lax.slice_in_dim(block, 0, width, axis=dim), axis, backward)
        block = jnp.concatenate([low, block, high], axis=dim)
    return block


def combine_partial(first_part, second_part):
    out_first, lse_first = first_part
    out_second, lse_second = second_part
    width = out_first.shape[1] // lse_first.shape[0]
    joint = jnp.logaddexp(lse_first, lse_second)
    share_first = jnp.repeat(jnp.exp(lse_first - joint).T, width, axis=1)
    share_second = jnp.repeat(jnp.exp(lse_second - joint).T, width, axis=1)
    return (out_first * share_first + out_second * share_second, joint)


def body(
    span_frames,
    query_rows,
    key_rows,
    context_frames,
    key_mask,
    value_weight,
    out_weight,
    expand_weight,
    depth_weight,
    norm_scale,
    norm_shift,
    project_weight,
):
    width = key_rows.shape[1]
    head_dim = width // HEADS
    scale = 1.0 / math.sqrt(head_dim)
    values = jnp.dot(context_frames, value_weight, preferred_element_type=jnp.float32).astype(
        jnp.bfloat16
    )
    key_heads = key_rows.reshape(key_rows.shape[0], HEADS, head_dim)
    value_heads = values.reshape(values.shape[0], HEADS, head_dim)
    valid = key_mask > 0
    gathered = lax.all_gather(query_rows, "seq", axis=0, tiled=True)
    own_rows = query_rows.shape[0]
    total_rows = gathered.shape[0]
    block = min(512, total_rows)
    blocks = total_rows // block
    query_blocks = gathered.reshape(blocks, block, HEADS, head_dim)

    def block_scores(query_block):
        scores = (
            jnp.einsum("bhd,khd->hbk", query_block, key_heads, preferred_element_type=jnp.float32)
            * scale
        )
        return jnp.where(valid[None, None, :], scores, -1e30)

    def weighted(scores, shift_rows):
        weights = jnp.exp(scores - shift_rows[:, :, None])
        total = jnp.sum(weights, axis=2)
        numer = jnp.einsum(
            "hbk,khd->bhd",
            weights.astype(jnp.bfloat16),
            value_heads,
            preferred_element_type=jnp.float32,
        )
        return (numer.reshape(numer.shape[0], width), total)

    def merged_block(query_block):
        scores = block_scores(query_block)
        top = jnp.max(scores, axis=2)
        numer, total = weighted(scores, top)
        partial_value = numer / jnp.repeat(total.T, head_dim, axis=1)
        partial_lse = top + jnp.log(total)
        return combined_all((partial_value, partial_lse), "seq", combine_partial)

    merged, merged_lse = lax.map(merged_block, query_blocks)
    merged = merged.reshape(total_rows, width)
    first_row = lax.axis_index("seq") * own_rows
    attended = lax.dynamic_slice_in_dim(merged, first_row, own_rows, 0).astype(jnp.bfloat16)
    wide = span_frames.astype(jnp.float32) + jnp.dot(
        attended, out_weight, preferred_element_type=jnp.float32
    )
    mixed = wide.astype(jnp.bfloat16)
    stream = mixed.astype(jnp.float32)
    centre = jnp.mean(stream, axis=1, keepdims=True)
    spread = jnp.mean((stream - centre) ** 2, axis=1, keepdims=True)
    normed = ((stream - centre) / jnp.sqrt(spread + 1e-05)).astype(jnp.bfloat16)
    expanded = jnp.dot(normed, expand_weight, preferred_element_type=jnp.float32)
    gated = (expanded[:, :width] * jax.nn.sigmoid(expanded[:, width:])).astype(jnp.bfloat16)
    reach = depth_weight.shape[0] // 2
    padded = with_halo(gated, (("seq", 0),), reach).astype(jnp.float32)
    conv = jnp.zeros((own_rows, width), jnp.float32)
    for offset in range(depth_weight.shape[0]):
        conv = conv + padded[offset : offset + own_rows] * depth_weight[offset][None, :]
    normal_conv = conv * norm_scale[None, :] + norm_shift[None, :]
    activated = (normal_conv * jax.nn.sigmoid(normal_conv)).astype(jnp.bfloat16)
    return (stream + jnp.dot(activated, project_weight, preferred_element_type=jnp.float32)).astype(
        jnp.bfloat16
    )


def solution(mesh):
    in_specs = (
        P(("groups", "seq"), None),
        P(("groups", "seq"), None),
        P(("groups", "seq"), None),
        P(("groups", "seq"), None),
        P(("groups", "seq")),
        P(),
        P(),
        P(),
        P(),
        P(),
        P(),
        P(),
    )
    out_specs = P(("groups", "seq"), None)
    return jax.shard_map(body, mesh=mesh, in_specs=in_specs, out_specs=out_specs, check_vma=False)
```

profile of v0, /device:TPU:3, one launch (start us, length us, event | category | flops | bytes accessed | tf_op | source)
XLA Modules:
  0.0 159.9 jit_solution(10683933736203446552)
XLA Ops:
  7.3 19.4 %all_gather.15 = bf16[256,512]{1,0:T(8,128)(2,1)S(1)} all-gather(bf16[16,512]{1,0:T(8,128)(2,1)} %param.15), channel_id=1, replica_groups=mesh['groups'=2,'seq'=16] {'seq'}, dimensions={0}, use_global_device_ids=true | all-gather | bytes 278528 | tf_op jit(solution)/shard_map/all_gather | solution.py:64
  26.8 1.3 copy.21
  29.0 1.2 fusion.6
  30.7 1.1 fusion.17
  32.9 22.3 %all-gather = f32[128,256]{1,0:T(8,128)S(1)} all-gather(f32[8,256]{1,0:T(8,128)S(1)} %log_add_fusion), channel_id=2, replica_groups=mesh['groups'=2,'seq'=16] {'seq'}, dimensions={0}, use_global_device_ids=true | all-gather | bytes 139264 | tf_op jit(solution)/shard_map/while/body/eval_jaxpr/all_gather | solution.py:11
  55.2 52.4 %all-gather.3.cloned.1.call-done = f32[16,256,512]{2,1,0:T(8,128)} async-done(((f32[1,256,512]{2,1,0:T(8,128)}), f32[16,256,512]{2,1,0:T(8,128)}) %all-gather.3.cloned.1.call-update) | async-done | bytes 8388624 | tf_op jit(solution)/shard_map/while/body/eval_jaxpr/all_gather | solution.py:11
  108.9 7.6 %slice.289 = f32[15,256,512]{2,1,0:T(8,128)} slice(f32[16,256,512]{2,1,0:T(8,128)} %all-gather.3.cloned.1.call-done), slice={[1:16], [0:256], [0:512]} | slice | bytes 15728640 | tf_op jit(solution)/shard_map/while/body/eval_jaxpr/slice | solution.py:13
  116.5 23.7 %while.19 = (s32[]{:T(128)}, f32[256,512]{0,1:T(8,128)S(1)}, f32[8,256]{1,0:T(8,128)S(1)}, f32[15,8,256]{2,1,0:T(8,128)S(1)}, f32[15,256,512]{2,1,0:T(8,128)}, /*index=5*/s32[]{:T(128)}) while((s32[]{:T(128)}, f32[256,512]{0,1:T(8,128)S(1)}, f32[8,256]{1,0:T(8,128)S(1)}, f32[15,8,256]{2,1,0:T(8,128)S(1)}, f32[15,256,512]{2,1,0:T(8,128)}, ...), condition=%wide.region_3.4_spmd, body=%wide.region_2.3_spmd.sunk | while | flops 413698 | bytes 3743825 | solution.py:14
  116.6 1.1 constant_dynamic-slice_fusion.2
  118.2 1.1 constant_dynamic-slice_fusion.2
  119.8 1.1 constant_dynamic-slice_fusion.2
  121.3 1.1 constant_dynamic-slice_fusion.2
  122.9 1.1 constant_dynamic-slice_fusion.2
  126.1 1.1 constant_dynamic-slice_fusion.2
  127.6 1.1 constant_dynamic-slice_fusion.2
  129.2 1.1 constant_dynamic-slice_fusion.2
  130.8 1.1 constant_dynamic-slice_fusion.2
  135.5 1.1 constant_dynamic-slice_fusion.2
  137.1 1.1 constant_dynamic-slice_fusion.2
  138.7 1.1 constant_dynamic-slice_fusion.2
  141.2 3.9 %collective-permute-start = (bf16[15,512]{1,0:T(8,128)(2,1)S(1)}, bf16[15,512]{1,0:T(8,128)(2,1)S(1)}, u32[]{:S(2)}, u32[]{:S(2)}) collective-permute-start(bf16[15,512]{1,0:T(8,128)(2,1)S(1)} %get-tuple-element.99), channel_id=1, source_target_pairs={{0,1},{1,2},{2,3},{3,4},{4,5},{5,6},{6,7},{7,8},{8,9},{9,10},{10,1... | collective-permute-start | bytes 46088 | tf_op jit(solution)/shard_map/ppermute | solution.py:23
  145.1 1.9 %collective-permute-start.1 = (bf16[15,512]{1,0:T(8,128)(2,1)S(1)}, bf16[15,512]{1,0:T(8,128)(2,1)S(1)}, u32[]{:S(2)}, u32[]{:S(2)}) collective-permute-start(bf16[15,512]{1,0:T(8,128)(2,1)S(1)} %get-tuple-element.100), channel_id=1, source_target_pairs={{1,0},{2,1},{3,2},{4,3},{5,4},{6,5},{7,6},{8,7},{9,8},{10,9},{11,1... | collective-permute-start | bytes 46088 | tf_op jit(solution)/shard_map/ppermute | solution.py:26
  147.0 4.0 %collective-permute-done.1 = bf16[15,512]{1,0:T(8,128)(2,1)S(1)} collective-permute-done((bf16[15,512]{1,0:T(8,128)(2,1)S(1)}, bf16[15,512]{1,0:T(8,128)(2,1)S(1)}, u32[]{:S(2)}, u32[]{:S(2)}) %collective-permute-start.1) | collective-permute-done | bytes 15392 | tf_op jit(solution)/shard_map/ppermute | solution.py:26
  151.1 2.0 %fusion.16 = bf16[16,512]{1,0:T(8,128)(2,1)} fusion(f32[16,512]{1,0:T(8,128)S(1)} %get-tuple-element.104, bf16[512,512]{1,0:T(8,128)(2,1)} %param.25, f32[46,512]{1,0:T(8,128)S(1)} %maximum_convert_fusion, f32[512]{0:T(512)S(1)} %copy-done.6, f32[512]{0:T(512)S(1)} %copy-done.7, f32[512]{0:T(512)S(1)} %bitcast.130, f32[512]{0:T(512)S(1)} %bitcast.131, ...), kind=kOutput, calls=%fused_computation.26 | convolution fusion | flops 8962048 | bytes 1656832 | tf_op jit(solution)/shard_map/dot_general | solution.py:118
  (102 shorter events, 15.6 us)
Async XLA Ops:
  6.5 134.3 %copy-start = (bf16[512,1024]{1,0:T(8,128)(2,1)S(1)}, bf16[512,1024]{1,0:T(8,128)(2,1)}, u32[]{:S(2)}) copy-start(bf16[512,1024]{1,0:T(8,128)(2,1)} %param.21) | copy-start | bytes 3145732
  6.5 101.1 %all-gather.3.cloned.1.call-start = ((), (), s32[]{:S(2)}) async-start(), calls=%async_computation | async-start | bytes 8912896 | tf_op jit(solution)/shard_map/while/body/eval_jaxpr/all_gather | solution.py:11
  28.1 2.1 %copy-start.1 = (bf16[512,512]{1,0:T(8,128)(2,1)S(1)}, bf16[512,512]{1,0:T(8,128)(2,1)}, u32[]{:S(2)}) copy-start(bf16[512,512]{1,0:T(8,128)(2,1)} %param.17) | copy-start | bytes 1572868
  28.1 2.1 %copy-start.2 = (bf16[512,512]{1,0:T(8,128)(2,1)S(1)}, bf16[512,512]{1,0:T(8,128)(2,1)}, u32[]{:S(2)}) copy-start(bf16[512,512]{1,0:T(8,128)(2,1)} %param.19) | copy-start | bytes 1572868
  30.7 24.5 %copy-start.4 = (f32[31,512]{1,0:T(8,128)S(1)}, f32[31,512]{1,0:T(8,128)}, u32[]{:S(2)}) copy-start(f32[31,512]{1,0:T(8,128)} %param.22) | copy-start | bytes 190468
  116.5 23.7 %copy-start.3 = (bf16[512,512]{1,0:T(8,128)(2,1)S(1)}, bf16[512,512]{1,0:T(8,128)(2,1)}, u32[]{:S(2)}) copy-start(bf16[512,512]{1,0:T(8,128)(2,1)} %param.20) | copy-start | bytes 1572868
  116.5 23.7 %copy-start.5 = (bf16[16,512]{1,0:T(8,128)(2,1)S(1)}, bf16[16,512]{1,0:T(8,128)(2,1)}, u32[]{:S(2)}) copy-start(bf16[16,512]{1,0:T(8,128)(2,1)} %param.14) | copy-start | bytes 49156
  116.5 34.6 %copy-start.6 = (f32[512]{0:T(512)S(1)}, f32[512]{0:T(512)}, u32[]{:S(2)}) copy-start(f32[512]{0:T(512)} %param.24) | copy-start | bytes 6148
  116.5 34.6 %copy-start.7 = (f32[512]{0:T(512)S(1)}, f32[512]{0:T(512)}, u32[]{:S(2)}) copy-start(f32[512]{0:T(512)} %param.23) | copy-start | bytes 6148
  141.2 5.9 %collective-permute-start = (bf16[15,512]{1,0:T(8,128)(2,1)S(1)}, bf16[15,512]{1,0:T(8,128)(2,1)S(1)}, u32[]{:S(2)}, u32[]{:S(2)}) collective-permute-start(bf16[15,512]{1,0:T(8,128)(2,1)S(1)} %get-tuple-element.99), channel_id=1, source_target_pairs={{0,1},{1,2},{2,3},{3,4},{4,5},{5,6},{6,7},{7,8},{8,9},{9,10},{10,1... | collective-permute-start | bytes 46088 | tf_op jit(solution)/shard_map/ppermute | solution.py:23
  145.1 6.0 %collective-permute-start.1 = (bf16[15,512]{1,0:T(8,128)(2,1)S(1)}, bf16[15,512]{1,0:T(8,128)(2,1)S(1)}, u32[]{:S(2)}, u32[]{:S(2)}) collective-permute-start(bf16[15,512]{1,0:T(8,128)(2,1)S(1)} %get-tuple-element.100), channel_id=1, source_target_pairs={{1,0},{2,1},{3,2},{4,3},{5,4},{6,5},{7,6},{8,7},{9,8},{10,9},{11,1... | collective-permute-start | bytes 46088 | tf_op jit(solution)/shard_map/ppermute | solution.py:26
Sparse Core Ops, SparseCore 0:
  33.0 74.5 all-gather.2
where the time goes:
time: 161 us; the launch traced here: 160 us
  waiting for transfers between devices  56.4 us (35%)
  blocking collectives  41.6 us (26%)
  local copies, waits for them, and re-layouts  30.6 us (19%)
  between operations  13.6 us (8%)
  other arithmetic  6.08 us (4%)
  starting transfers between devices  5.84 us (4%)
  matrix products  5.07 us (3%)
    all_gather x1, waiting for transfers between devices, combined_all(): pieces = jax.tree.map(lambda part: lax.all_gather(part, axis), value)  52.4 us
    all_gather x1, blocking collectives, combined_all(): pieces = jax.tree.map(lambda part: lax.all_gather(part, axis), value)  22.3 us
    all_gather x1, blocking collectives, body(): gathered = lax.all_gather(query_rows, 'seq', axis=0, tiled=True)  19.4 us
    dynamic_slice x30, local copies, waits for them, and re-layouts, combined_all(): lax.scan(lambda so_far, section: (join(so_far, section), None), head, tail)  19.2 us
    slice x2, local copies, waits for them, and re-layouts, combined_all(): tail = jax.tree.map(lambda part: part[1:], pieces)  7.61 us
    ppermute x1, waiting for transfers between devices, with_halo(): lax.ppermute(lax.slice_in_dim(block, 0, width, axis=dim), axis, backward)  3.99 us
    ppermute x1, starting transfers between devices, with_halo(): lax.ppermute(lax.slice_in_dim(block, block.shape[dim] - width, None, axis...  3.91 us
    add x15, other arithmetic, combine_partial(): return (out_first * share_first + out_second * share_second, joint)  3.24 us
  transfers between devices with their start and end apart: 3, of which 2 were waited for; matrix products, arithmetic and copies ran while one was open for 0% of the time, Pallas kernels for 0%

commit v1 on v0

--- a/solution.py
+++ b/solution.py
@@ -5,6 +5,12 @@
 from jax.sharding import PartitionSpec as P
 
 HEADS = 8
+
+
+def gather_from_all(x, axis, dim):
+    peers = lax.axis_size(axis)
+    repeats = [peers if d == dim else 1 for d in range(x.ndim)]
+    return lax.all_to_all(jnp.tile(x, repeats), axis, split_axis=dim, concat_axis=dim, tiled=True)
 
 
 def combined_all(value, axis, join):
@@ -61,7 +67,7 @@
     key_heads = key_rows.reshape(key_rows.shape[0], HEADS, head_dim)
     value_heads = values.reshape(values.shape[0], HEADS, head_dim)
     valid = key_mask > 0
-    gathered = lax.all_gather(query_rows, "seq", axis=0, tiled=True)
+    gathered = gather_from_all(query_rows, "seq", 0)
     own_rows = query_rows.shape[0]
     total_rows = gathered.shape[0]
     block = min(512, total_rows)

time: 161 us -> 155 us (0.963)
  blocking collectives: 41.6 us -> 19.8 us
  starting transfers between devices: 5.84 us -> 12.5 us
  waiting for transfers between devices: 56.4 us -> 62.2 us
  local copies, waits for them, and re-layouts: 30.6 us -> 32.3 us
    all_gather x1 -> x0, blocking collectives: 19.4 us -> none  [body(): gathered = lax.all_gather(query_rows, 'seq', axis=0, tiled=True)]
    all_to_all x0 -> x1, starting transfers between devices: none -> 6.63 us  [gather_from_all(): lax.all_to_all(jnp.tile(x, repeats), axis, split_axis=dim, concat_axis=di...]
    all_to_all x0 -> x1, waiting for transfers between devices: none -> 4.82 us  [gather_from_all(): lax.all_to_all(jnp.tile(x, repeats), axis, split_axis=dim, concat_axis=di...]
    all_gather x1, blocking collectives: 22.3 us -> 19.8 us  [combined_all(): pieces = jax.tree.map(lambda part: lax.all_gather(part, axis), value)]
  transfers between devices with their start and end apart: 3 -> 4, of which waited for: 2 -> 3; matrix products, arithmetic and copies ran while one was open for 0% -> 2% of each run, Pallas kernels for 0% -> 0%
where the time goes in v1:
time: 155 us; the launch traced here: 153 us
  waiting for transfers between devices  62.2 us (40%)
  local copies, waits for them, and re-layouts  32.3 us (21%)
  blocking collectives  19.8 us (13%)
  between operations  13.6 us (9%)
  starting transfers between devices  12.5 us (8%)
  matrix products  6.22 us (4%)
  other arithmetic  6.07 us (4%)
    all_gather x1, waiting for transfers between devices, combined_all(): pieces = jax.tree.map(lambda part: lax.all_gather(part, axis), value)  53.4 us
    all_gather x1, blocking collectives, combined_all(): pieces = jax.tree.map(lambda part: lax.all_gather(part, axis), value)  19.8 us
    dynamic_slice x30, local copies, waits for them, and re-layouts, combined_all(): lax.scan(lambda so_far, section: (join(so_far, section), None), head, tail)  19.2 us
    slice x2, local copies, waits for them, and re-layouts, combined_all(): tail = jax.tree.map(lambda part: part[1:], pieces)  7.61 us
    all_to_all x1, starting transfers between devices, gather_from_all(): lax.all_to_all(jnp.tile(x, repeats), axis, split_axis=dim, concat_axis=di...  6.63 us
    all_to_all x1, waiting for transfers between devices, gather_from_all(): lax.all_to_all(jnp.tile(x, repeats), axis, split_axis=dim, concat_axis=di...  4.82 us
    ppermute x1, waiting for transfers between devices, with_halo(): lax.ppermute(lax.slice_in_dim(block, 0, width, axis=dim), axis, backward)  3.99 us
    ppermute x1, starting transfers between devices, with_halo(): lax.ppermute(lax.slice_in_dim(block, block.shape[dim] - width, None, axis...  3.91 us
  transfers between devices with their start and end apart: 4, of which 3 were waited for; matrix products, arithmetic and copies ran while one was open for 2% of the time, Pallas kernels for 0%

profile of v1, /device:TPU:3, one launch (start us, length us, event | category | flops | bytes accessed | tf_op | source)
XLA Modules:
  0.0 153.3 jit_solution(7608614088011907402)
XLA Ops:
  6.5 1.5 tile.2
  8.1 6.6 %all-to-all-start = ((bf16[16,16,512]{2,1,0:T(8,128)(2,1)}), bf16[16,16,512]{2,1,0:T(8,128)(2,1)S(1)}, u32[]{:S(2)}, u32[]{:S(2)}) async-start(bf16[16,16,512]{2,1,0:T(8,128)(2,1)} %tile.2), calls=%async_computation | async-start | bytes 524288 | tf_op jit(solution)/shard_map/all_to_all | solution.py:13
  14.7 1.3 copy.20
  16.7 1.7 %convolution_convert_fusion = bf16[512,512]{0,1:T(8,128)(2,1)S(1)} fusion(bf16[512,512]{1,0:T(8,128)(2,1)} %param.17, bf16[512,512]{1,0:T(8,128)(2,1)} %param.19), kind=kOutput, calls=%fused_computation.20 | convolution fusion | flops 268697600 | bytes 1572864 | tf_op jit(solution)/shard_map/dot_general | solution.py:64
  18.4 4.8 %all-to-all-done = bf16[16,16,512]{2,1,0:T(8,128)(2,1)S(1)} async-done(((bf16[16,16,512]{2,1,0:T(8,128)(2,1)}), bf16[16,16,512]{2,1,0:T(8,128)(2,1)S(1)}, u32[]{:S(2)}, u32[]{:S(2)}) %all-to-all-start) | async-done | bytes 262176 | tf_op jit(solution)/shard_map/all_to_all | solution.py:13
  24.2 1.3 fusion.6
  25.6 1.1 fusion.17
  27.8 19.8 %all-gather = f32[128,256]{1,0:T(8,128)S(1)} all-gather(f32[8,256]{1,0:T(8,128)S(1)} %log_add_fusion), channel_id=2, replica_groups=mesh['groups'=2,'seq'=16] {'seq'}, dimensions={0}, use_global_device_ids=true | all-gather | bytes 139264 | tf_op jit(solution)/shard_map/while/body/eval_jaxpr/all_gather | solution.py:17
  47.6 53.4 %all-gather.3.cloned.1.call-done = f32[16,256,512]{2,1,0:T(8,128)} async-done(((f32[1,256,512]{2,1,0:T(8,128)}), f32[16,256,512]{2,1,0:T(8,128)}) %all-gather.3.cloned.1.call-update) | async-done | bytes 8388624 | tf_op jit(solution)/shard_map/while/body/eval_jaxpr/all_gather | solution.py:17
  102.3 7.6 %slice.289 = f32[15,256,512]{2,1,0:T(8,128)} slice(f32[16,256,512]{2,1,0:T(8,128)} %all-gather.3.cloned.1.call-done), slice={[1:16], [0:256], [0:512]} | slice | bytes 15728640 | tf_op jit(solution)/shard_map/while/body/eval_jaxpr/slice | solution.py:19
  109.9 23.7 %while.19 = (s32[]{:T(128)}, f32[256,512]{0,1:T(8,128)S(1)}, f32[8,256]{1,0:T(8,128)S(1)}, f32[15,8,256]{2,1,0:T(8,128)S(1)}, f32[15,256,512]{2,1,0:T(8,128)}, /*index=5*/s32[]{:T(128)}) while((s32[]{:T(128)}, f32[256,512]{0,1:T(8,128)S(1)}, f32[8,256]{1,0:T(8,128)S(1)}, f32[15,8,256]{2,1,0:T(8,128)S(1)}, f32[15,256,512]{2,1,0:T(8,128)}, ...), condition=%wide.region_3.4_spmd, body=%wide.region_2.3_spmd.sunk | while | flops 413698 | bytes 3743825 | solution.py:20
  110.0 1.1 constant_dynamic-slice_fusion.2
  113.2 1.1 constant_dynamic-slice_fusion.2
  114.8 1.1 constant_dynamic-slice_fusion.2
  116.3 1.1 constant_dynamic-slice_fusion.2
  122.6 1.1 constant_dynamic-slice_fusion.2
  124.2 1.1 constant_dynamic-slice_fusion.2
  125.8 1.1 constant_dynamic-slice_fusion.2
  127.4 1.1 constant_dynamic-slice_fusion.2
  132.1 1.1 constant_dynamic-slice_fusion.2
  134.6 3.9 %collective-permute-start = (bf16[15,512]{1,0:T(8,128)(2,1)S(1)}, bf16[15,512]{1,0:T(8,128)(2,1)S(1)}, u32[]{:S(2)}, u32[]{:S(2)}) collective-permute-start(bf16[15,512]{1,0:T(8,128)(2,1)S(1)} %get-tuple-element.99), channel_id=1, source_target_pairs={{0,1},{1,2},{2,3},{3,4},{4,5},{5,6},{6,7},{7,8},{8,9},{9,10},{10,1... | collective-permute-start | bytes 46088 | tf_op jit(solution)/shard_map/ppermute | solution.py:29
  138.5 1.9 %collective-permute-start.1 = (bf16[15,512]{1,0:T(8,128)(2,1)S(1)}, bf16[15,512]{1,0:T(8,128)(2,1)S(1)}, u32[]{:S(2)}, u32[]{:S(2)}) collective-permute-start(bf16[15,512]{1,0:T(8,128)(2,1)S(1)} %get-tuple-element.100), channel_id=1, source_target_pairs={{1,0},{2,1},{3,2},{4,3},{5,4},{6,5},{7,6},{8,7},{9,8},{10,9},{11,1... | collective-permute-start | bytes 46088 | tf_op jit(solution)/shard_map/ppermute | solution.py:32
  140.5 4.0 %collective-permute-done.1 = bf16[15,512]{1,0:T(8,128)(2,1)S(1)} collective-permute-done((bf16[15,512]{1,0:T(8,128)(2,1)S(1)}, bf16[15,512]{1,0:T(8,128)(2,1)S(1)}, u32[]{:S(2)}, u32[]{:S(2)}) %collective-permute-start.1) | collective-permute-done | bytes 15392 | tf_op jit(solution)/shard_map/ppermute | solution.py:32
  144.5 2.0 %fusion.16 = bf16[16,512]{1,0:T(8,128)(2,1)} fusion(f32[16,512]{1,0:T(8,128)S(1)} %get-tuple-element.104, bf16[512,512]{1,0:T(8,128)(2,1)} %param.25, f32[46,512]{1,0:T(8,128)S(1)} %maximum_convert_fusion, f32[512]{0:T(512)S(1)} %copy-done.4, f32[512]{0:T(512)S(1)} %copy-done.5, f32[512]{0:T(512)S(1)} %bitcast.127, f32[512]{0:T(512)S(1)} %bitcast.128, ...), kind=kOutput, calls=%fused_computation.26 | convolution fusion | flops 8962048 | bytes 1656832 | tf_op jit(solution)/shard_map/dot_general | solution.py:124
  (100 shorter events, 18.4 us)
Async XLA Ops:
  6.5 127.7 %copy-start = (bf16[512,1024]{1,0:T(8,128)(2,1)S(1)}, bf16[512,1024]{1,0:T(8,128)(2,1)}, u32[]{:S(2)}) copy-start(bf16[512,1024]{1,0:T(8,128)(2,1)} %param.21) | copy-start | bytes 3145732
  8.1 15.1 %all-to-all-start = ((bf16[16,16,512]{2,1,0:T(8,128)(2,1)}), bf16[16,16,512]{2,1,0:T(8,128)(2,1)S(1)}, u32[]{:S(2)}, u32[]{:S(2)}) async-start(bf16[16,16,512]{2,1,0:T(8,128)(2,1)} %tile.2), calls=%async_computation | async-start | bytes 524288 | tf_op jit(solution)/shard_map/all_to_all | solution.py:13
  14.7 86.4 %all-gather.3.cloned.1.call-start = ((), (), s32[]{:S(2)}) async-start(), calls=%async_computation.1 | async-start | bytes 8912896 | tf_op jit(solution)/shard_map/while/body/eval_jaxpr/all_gather | solution.py:17
  25.6 2.2 %copy-start.2 = (f32[31,512]{1,0:T(8,128)S(1)}, f32[31,512]{1,0:T(8,128)}, u32[]{:S(2)}) copy-start(f32[31,512]{1,0:T(8,128)} %param.22) | copy-start | bytes 190468
  109.9 23.7 %copy-start.1 = (bf16[512,512]{1,0:T(8,128)(2,1)S(1)}, bf16[512,512]{1,0:T(8,128)(2,1)}, u32[]{:S(2)}) copy-start(bf16[512,512]{1,0:T(8,128)(2,1)} %param.20) | copy-start | bytes 1572868
  109.9 23.7 %copy-start.3 = (bf16[16,512]{1,0:T(8,128)(2,1)S(1)}, bf16[16,512]{1,0:T(8,128)(2,1)}, u32[]{:S(2)}) copy-start(bf16[16,512]{1,0:T(8,128)(2,1)} %param.14) | copy-start | bytes 49156
  109.9 34.6 %copy-start.4 = (f32[512]{0:T(512)S(1)}, f32[512]{0:T(512)}, u32[]{:S(2)}) copy-start(f32[512]{0:T(512)} %param.24) | copy-start | bytes 6148
  109.9 34.6 %copy-start.5 = (f32[512]{0:T(512)S(1)}, f32[512]{0:T(512)}, u32[]{:S(2)}) copy-start(f32[512]{0:T(512)} %param.23) | copy-start | bytes 6148
  134.6 5.9 %collective-permute-start = (bf16[15,512]{1,0:T(8,128)(2,1)S(1)}, bf16[15,512]{1,0:T(8,128)(2,1)S(1)}, u32[]{:S(2)}, u32[]{:S(2)}) collective-permute-start(bf16[15,512]{1,0:T(8,128)(2,1)S(1)} %get-tuple-element.99), channel_id=1, source_target_pairs={{0,1},{1,2},{2,3},{3,4},{4,5},{5,6},{6,7},{7,8},{8,9},{9,10},{10,1... | collective-permute-start | bytes 46088 | tf_op jit(solution)/shard_map/ppermute | solution.py:29
  138.5 6.0 %collective-permute-start.1 = (bf16[15,512]{1,0:T(8,128)(2,1)S(1)}, bf16[15,512]{1,0:T(8,128)(2,1)S(1)}, u32[]{:S(2)}, u32[]{:S(2)}) collective-permute-start(bf16[15,512]{1,0:T(8,128)(2,1)S(1)} %get-tuple-element.100), channel_id=1, source_target_pairs={{1,0},{2,1},{3,2},{4,3},{5,4},{6,5},{7,6},{8,7},{9,8},{10,9},{11,1... | collective-permute-start | bytes 46088 | tf_op jit(solution)/shard_map/ppermute | solution.py:32
Sparse Core Ops, SparseCore 0:
  27.9 73.1 all-gather.2
